TPU v7x, 256 devices: a whole 4x4x8 slice. The times are simulated.
256 devices in a mesh: dp: 128 (over x, z, y), rep: 2 (over core).
Axes of the slice: x: 4, y: 4, z: 8, core: 2. Of those that a mesh axis runs over, the one named last changes fastest.
Arguments:
- features: bfloat16 [32768, 1024], P(('dp', 'rep')), may hold values from -6 to 6
- cotangent: bfloat16 [32768, 1024], P(('dp', 'rep')), may hold values from -6 to 6
- routes: int32 [32768, 2], P(('dp', 'rep')), may hold values from 0 to 127, all different within a row; in each aligned block of 128 rows (0 to 127, 128 to 255, ...) at most 3 rows name the same one
- route_weights: float32 [32768, 2], P(('dp', 'rep')), may hold values from 0.2 to 1
- counts: int32 [32768], P(('dp', 'rep')), may hold values from 1 to 4
- cross_weight: bfloat16 [1024, 1024], P(('dp', 'rep')), may hold values from -0.1875 to 0.1875
- gate_weight: bfloat16 [1024, 1024], P(('dp', 'rep')), may hold values from -0.1875 to 0.1875
- cross_bias: float32 [1024], replicated, may hold values from -3 to 3
- gate_bias: float32 [1024], replicated, may hold values from -4 to 4
- expert_in: bfloat16 [128, 1024, 2048], P('dp', None, 'rep'), may hold values from -0.1875 to 0.1875
- expert_out: bfloat16 [128, 2048, 1024], P('dp', 'rep'), may hold values from -0.125 to 0.125
Outputs:
- layer_output: bfloat16 [32768, 1024], P(('dp', 'rep'))
- grad_cross_weight: bfloat16 [1024, 1024], P('rep')
- grad_gate_weight: bfloat16 [1024, 1024], P('rep')
- grad_cross_bias: float32 [1024], P('rep')
- grad_gate_bias: float32 [1024], P('rep')
- grad_expert_in: bfloat16 [128, 1024, 2048], P('dp', None, 'rep')
- grad_expert_out: bfloat16 [128, 2048, 1024], P('dp', 'rep')
Inputs may be any that keep to these rules, and one draw needn't show every extreme that they name: `routes`: the two experts of a row differ. In the rows of one device (aligned blocks of 128 rows) no expert is named more than 3 times, and in every draw some expert is named exactly 3 times in some block. Every expert is named by some row.
All inputs are finite; a program needn't handle non-finite values.
Results may differ from a plain program's by a relative error of at most 0.02.
Values may be sent and summed in bfloat16 or wider, within the bound.
No kernel may reach another device: no remote copies, remote signals or barrier semaphores. Data moves between devices by JAX's collectives and lax.ppermute only.
A program may use at most 128 MiB of HBM per device.

v0:
```python
import jax
import jax.numpy as jnp
from jax import lax
from jax.sharding import PartitionSpec as P


def slot_layout(routes, experts_n, capacity):
    flat_routes = routes.reshape(-1)
    onehot = (flat_routes[:, None] == jnp.arange(experts_n, dtype=jnp.int32)[None, :]).astype(
        jnp.int32
    )
    position = jnp.sum((jnp.cumsum(onehot, axis=0) - 1) * onehot, axis=1)
    slot_index = flat_routes * capacity + position
    slot_ids = jnp.arange(experts_n * capacity, dtype=jnp.int32)
    slot_match = (slot_index[None, :] == slot_ids[:, None]).astype(jnp.bfloat16)
    return (slot_index, slot_match)


def body(
    features,
    cotangent,
    routes,
    route_weights,
    counts,
    cross_weight,
    gate_weight,
    cross_bias,
    gate_bias,
    expert_in,
    expert_out,
):
    row_count, width = features.shape
    experts_n = lax.axis_size("dp")
    capacity = max(2, 3 * row_count // experts_n)
    feature_f = features.astype(jnp.float32)
    cross_acc = jnp.dot(
        features,
        lax.all_gather(cross_weight, ("dp", "rep"), axis=0, tiled=True),
        preferred_element_type=jnp.float32,
    )
    gate_acc = jnp.dot(
        features,
        lax.all_gather(gate_weight, ("dp", "rep"), axis=0, tiled=True),
        preferred_element_type=jnp.float32,
    )
    cross_term = cross_acc + cross_bias
    gate_term = jax.nn.sigmoid(gate_acc + gate_bias)
    crossed = (feature_f * cross_term * gate_term + feature_f).astype(jnp.bfloat16)
    slot_index, slot_match = slot_layout(routes, experts_n, capacity)
    row_match = jnp.sum(slot_match.reshape(experts_n * capacity, row_count, 2), axis=2)
    send_buffer = jnp.dot(row_match, crossed, preferred_element_type=jnp.float32).astype(
        jnp.bfloat16
    )
    send_buffer = send_buffer.reshape(experts_n, capacity, width)
    whole_in, whole_out = (
        lax.all_gather(expert_in, "rep", axis=2, tiled=True),
        lax.all_gather(expert_out, "rep", axis=1, tiled=True),
    )
    weight_in = whole_in[0]
    weight_out = whole_out[0]
    received = lax.all_to_all(send_buffer, "dp", split_axis=0, concat_axis=0, tiled=True)
    pre_act = jnp.einsum("skd,df->skf", received, weight_in, preferred_element_type=jnp.float32)
    hidden = (pre_act * jax.nn.sigmoid(pre_act)).astype(jnp.bfloat16)
    result = jnp.einsum("skf,fd->skd", hidden, weight_out, preferred_element_type=jnp.float32)
    expert_result, slot_inputs, pre_act, hidden = (
        result.astype(jnp.bfloat16),
        received,
        pre_act,
        hidden,
    )
    returned = lax.all_to_all(expert_result, "dp", split_axis=0, concat_axis=0, tiled=True)
    gathered_out = (
        returned.reshape(experts_n * capacity, width)[slot_index]
        .reshape(row_count, 2, width)
        .astype(jnp.float32)
    )
    layer_output = (
        crossed.astype(jnp.float32) + jnp.sum(route_weights[:, :, None] * gathered_out, axis=1)
    ).astype(jnp.bfloat16)
    upstream = 0.05 * counts.astype(jnp.float32)[:, None] * cotangent.astype(jnp.float32)
    out_grad = (
        (route_weights[:, :, None] * upstream[:, None, :])
        .astype(jnp.bfloat16)
        .reshape(2 * row_count, width)
    )
    grad_send = jnp.dot(slot_match, out_grad, preferred_element_type=jnp.float32).astype(
        jnp.bfloat16
    )
    grad_send = grad_send.reshape(experts_n, capacity, width)
    grad_recv = lax.all_to_all(grad_send, "dp", split_axis=0, concat_axis=0, tiled=True)
    squash = jax.nn.sigmoid(pre_act)
    slope = squash * (1.0 + pre_act * (1.0 - squash))
    hid_grad = jnp.einsum("skd,fd->skf", grad_recv, weight_out, preferred_element_type=jnp.float32)
    pre_grad = (hid_grad * slope).astype(jnp.bfloat16)
    back_part = jnp.einsum("skf,df->skd", pre_grad, weight_in, preferred_element_type=jnp.float32)
    back_rows = back_part.astype(jnp.bfloat16)
    returned_grad = lax.all_to_all(back_rows, "dp", split_axis=0, concat_axis=0, tiled=True)
    grad_in_full = jnp.einsum(
        "skd,skf->df", slot_inputs, pre_grad, preferred_element_type=jnp.float32
    )
    grad_out_full = jnp.einsum("skf,skd->fd", hidden, grad_recv, preferred_element_type=jnp.float32)
    grad_in_part, grad_out_part = (
        lax.psum_scatter(
            grad_in_full[None].astype(jnp.bfloat16), "rep", scatter_dimension=2, tiled=True
        ).astype(jnp.float32),
        lax.psum_scatter(
            grad_out_full[None].astype(jnp.bfloat16), "rep", scatter_dimension=1, tiled=True
        ).astype(jnp.float32),
    )
    grad_expert_in = grad_in_part.astype(jnp.bfloat16)
    grad_expert_out = grad_out_part.astype(jnp.bfloat16)
    back_gathered = (
        returned_grad.reshape(experts_n * capacity, width)[slot_index]
        .reshape(row_count, 2, width)
        .astype(jnp.float32)
    )
    crossed_grad = upstream + jnp.sum(back_gathered, axis=1)
    cross_grad = (crossed_grad * feature_f * gate_term).astype(jnp.bfloat16)
    gate_grad = (crossed_grad * feature_f * cross_term * gate_term * (1.0 - gate_term)).astype(
        jnp.bfloat16
    )
    weight_cross = jnp.einsum("rd,re->de", features, cross_grad, preferred_element_type=jnp.float32)
    weight_gate = jnp.einsum("rd,re->de", features, gate_grad, preferred_element_type=jnp.float32)
    bias_cross = jnp.sum(cross_grad.astype(jnp.float32), axis=0)
    bias_gate = jnp.sum(gate_grad.astype(jnp.float32), axis=0)
    halves = (
        lax.psum_scatter(
            weight_cross.astype(jnp.bfloat16), "rep", scatter_dimension=0, tiled=True
        ).astype(jnp.float32),
        lax.psum_scatter(
            weight_gate.astype(jnp.bfloat16), "rep", scatter_dimension=0, tiled=True
        ).astype(jnp.float32),
        lax.psum_scatter(
            bias_cross.astype(jnp.bfloat16), "rep", scatter_dimension=0, tiled=True
        ).astype(jnp.float32),
        lax.psum_scatter(
            bias_gate.astype(jnp.bfloat16), "rep", scatter_dimension=0, tiled=True
        ).astype(jnp.float32),
    )
    summed = lax.psum((halves[0], halves[1], halves[2], halves[3]), "dp")
    return (
        layer_output,
        summed[0].astype(jnp.bfloat16),
        summed[1].astype(jnp.bfloat16),
        summed[2],
        summed[3],
        grad_expert_in,
        grad_expert_out,
    )


def solution(mesh):
    return jax.shard_map(
        body,
        mesh=mesh,
        in_specs=(
            P(("dp", "rep"), None),
            P(("dp", "rep"), None),
            P(("dp", "rep"), None),
            P(("dp", "rep"), None),
            P(("dp", "rep")),
            P(("dp", "rep"), None),
            P(("dp", "rep"), None),
            P(),
            P(),
            P("dp", None, "rep"),
            P("dp", "rep", None),
        ),
        out_specs=(
            P(("dp", "rep"), None),
            P("rep", None),
            P("rep", None),
            P("rep"),
            P("rep"),
            P("dp", None, "rep"),
            P("dp", "rep", None),
        ),
        check_vma=False,
    )
```

profile of v0, /device:TPU:0, one launch (start us, length us, event | category | flops | bytes accessed | tf_op | source)
XLA Modules:
  0.0 823.5 jit_solution(13755409493693492527)
XLA Ops:
  7.2 0.7 all-gather.11.cloned.1.call-update
  8.0 0.7 all-gather.13.cloned.1.call-update
  8.7 0.7 all-gather.7.cloned.1.call-update
  9.4 0.5 all-gather.9.cloned.1.call-update
  10.0 0.1 copy.58
  10.1 0.1 eq.49
  10.2 0.1 eq.45
  10.4 0.1 copy.61
  10.5 0.2 fusion.30
  10.8 0.2 fusion.31
  11.0 0.1 reduce_sum.68
  11.3 105.8 %all-gather.11.cloned.1.call-done = bf16[256,4,1024]{2,1,0:T(4,128)(2,1)} async-done(((bf16[1,4,1024]{2,1,0:T(4,128)(2,1)}), bf16[256,4,1024]{2,1,0:T(4,128)(2,1)}) %all-gather.11.cloned.1.call-update) | async-done | bytes 2097168 | tf_op jit(solution)/shard_map/all_gather | solution.py:38
  117.1 2.5 reshape.133
  119.7 104.3 %all-gather.13.cloned.1.call-done = bf16[256,4,1024]{2,1,0:T(4,128)(2,1)} async-done(((bf16[1,4,1024]{2,1,0:T(4,128)(2,1)}), bf16[256,4,1024]{2,1,0:T(4,128)(2,1)}) %all-gather.13.cloned.1.call-update) | async-done | bytes 2097168 | tf_op jit(solution)/shard_map/all_gather | solution.py:43
  223.9 3.9 reshape.135
  227.9 0.4 convolution_add_fusion.1
  228.4 3.1 fusion.25
  231.5 0.4 convolution_convert_fusion.1
  231.8 1.3 reshape.110
  233.1 11.8 %all-to-all-start = ((bf16[128,3,1024]{2,1,0:T(4,128)(2,1)}), bf16[128,3,1024]{2,1,0:T(4,128)(2,1)S(1)}, u32[]{:S(2)}, u32[]{:S(2)}) async-start(bf16[128,3,1024]{2,1,0:T(4,128)(2,1)} %reshape.110), calls=%async_computation | async-start | bytes 2097152 | tf_op jit(solution)/shard_map/all_to_all | solution.py:61
  245.0 0.1 copy.57
  245.2 0.4 mul.120
  245.6 0.7 mul.121
  246.3 0.1 mul.118
  246.5 0.5 convolution_convert_fusion
  246.9 1.3 reshape.112
  248.2 27.1 %all-to-all-done = bf16[128,3,1024]{2,1,0:T(4,128)(2,1)S(1)} async-done(((bf16[128,3,1024]{2,1,0:T(4,128)(2,1)}), bf16[128,3,1024]{2,1,0:T(4,128)(2,1)S(1)}, u32[]{:S(2)}, u32[]{:S(2)}) %all-to-all-start) | async-done | bytes 786464 | tf_op jit(solution)/shard_map/all_to_all | solution.py:61
  275.3 7.9 all-to-all-start.2
  283.2 0.8 copy.69
  284.1 5.7 fusion.6
  289.8 22.5 %all-to-all-done.2 = bf16[128,3,1024]{2,1,0:T(4,128)(2,1)} async-done(((bf16[128,3,1024]{2,1,0:T(4,128)(2,1)}), bf16[128,3,1024]{2,1,0:T(4,128)(2,1)}, u32[]{:S(2)}, u32[]{:S(2)}) %all-to-all-start.2) | async-done | bytes 786464 | tf_op jit(solution)/shard_map/all_to_all | solution.py:90
  312.3 5.9 multiply_convert_fusion
  318.3 1.8 fusion.12
  320.1 1.6 copy.68
  321.8 7.0 all-to-all-start.3
  328.7 0.3 reduce-scatter.5.cloned.1.call-start
  329.0 0.1 mul.110
  329.2 28.5 %all-to-all-done.3 = bf16[128,3,1024]{2,1,0:T(4,128)(2,1)S(1)} async-done(((bf16[128,3,1024]{2,1,0:T(4,128)(2,1)}), bf16[128,3,1024]{2,1,0:T(4,128)(2,1)S(1)}, u32[]{:S(2)}, u32[]{:S(2)}) %all-to-all-start.3) | async-done | bytes 786464 | tf_op jit(solution)/shard_map/all_to_all | solution.py:97
  357.7 0.7 reshape.113
  358.4 1.2 gather_fusion.1
  359.5 0.7 reshape.115
  360.2 1.2 reduce_sum.72
  361.5 1.4 fusion.35
  362.9 2.1 convert_bitcast_fusion.1
  365.0 2.1 convert_bitcast_fusion
  367.2 7.6 reduce-scatter.5.cloned.1.call-done
  374.7 19.3 %reduce-scatter.7.cloned.1.call-done = bf16[512,1024]{0,1:T(8,128)(2,1)} async-done(((bf16[1024,1024]{0,1:T(8,128)(2,1)}), bf16[512,1024]{0,1:T(8,128)(2,1)}) %reduce-scatter.7.cloned.1.call-update) | async-done | bytes 1048592 | tf_op jit(solution)/shard_map/reduce_scatter | solution.py:130
  394.1 3.9 fusion.8
  398.1 1.8 copy-done.2
  399.9 5.8 fusion.9
  405.7 4.0 fusion.15
  409.7 1.6 copy.65
  411.4 13.9 %all-to-all-start.1 = ((bf16[128,3,1024]{2,1,0:T(4,128)(2,1)}), bf16[128,3,1024]{2,1,0:T(4,128)(2,1)S(1)}, u32[]{:S(2)}, u32[]{:S(2)}) async-start(bf16[128,3,1024]{2,1,0:T(4,128)(2,1)} %copy.65), calls=%async_computation.1 | async-start | bytes 2097152 | tf_op jit(solution)/shard_map/all_to_all | solution.py:71
  425.3 0.6 dynamic-slice
  426.5 33.4 %all-to-all-done.1 = bf16[128,3,1024]{2,1,0:T(4,128)(2,1)S(1)} async-done(((bf16[128,3,1024]{2,1,0:T(4,128)(2,1)}), bf16[128,3,1024]{2,1,0:T(4,128)(2,1)S(1)}, u32[]{:S(2)}, u32[]{:S(2)}) %all-to-all-start.1) | async-done | bytes 786464 | tf_op jit(solution)/shard_map/all_to_all | solution.py:71
  459.9 0.7 reshape.111
  460.6 1.2 gather_fusion
  461.8 0.7 reshape.114
  462.5 2.5 all-reduce.4
  465.0 345.2 %all-reduce.2 = (f32[512]{0:T(512)}, f32[512]{0:T(512)}) all-reduce(f32[512]{0:T(512)S(1)} %get-tuple-element.52, f32[512]{0:T(512)S(1)} %get-tuple-element.51), channel_id=1, replica_groups=mesh['dp'=128,'rep'=2] {'dp'}, use_global_device_ids=true, to_apply=%region_12.13 | all-reduce | flops 1024 | bytes 8192 | tf_op jit(solution)/shard_map/psum | solution.py:140
  810.2 1.3 multiply_reduce_fusion
  811.6 0.8 add_convert_fusion
  812.4 2.3 copy.72
  814.7 2.3 copy.73
  (63 shorter events, 1.0 us)
Async XLA Ops:
  7.2 2.8 copy-start.9
  7.2 109.9 %all-gather.11.cloned.1.call-start = ((), (), s32[]{:S(2)}) async-start(), calls=%async_computation.14 | async-start | bytes 2105344 | tf_op jit(solution)/shard_map/all_gather | solution.py:38
  7.9 216.0 %all-gather.13.cloned.1.call-start = ((), (), s32[]{:S(2)}) async-start(), calls=%async_computation.15 | async-start | bytes 2105344 | tf_op jit(solution)/shard_map/all_gather | solution.py:43
  8.7 275.4 %all-gather.7.cloned.1.call-start = ((), (), s32[]{:S(2)}) async-start(), calls=%async_computation.8 | async-start | bytes 6291456 | tf_op jit(solution)/shard_map/all_gather | solution.py:56
  9.4 302.9 %all-gather.9.cloned.1.call-start = ((), (), s32[]{:S(2)}) async-start(), calls=%async_computation.9 | async-start | bytes 6291456 | tf_op jit(solution)/shard_map/all_gather | solution.py:57
  119.6 108.3 %copy-start.1 = (bf16[128,1024]{1,0:T(8,128)(2,1)S(1)}, bf16[128,1024]{1,0:T(8,128)(2,1)}, u32[]{:S(2)}) copy-start(bf16[128,1024]{1,0:T(8,128)(2,1)} %param.11) | copy-start | bytes 786436
  119.6 108.2 %copy-start.8 = (f32[1024]{0:T(1024)S(1)}, f32[1024]{0:T(1024)}, u32[]{:S(2)}) copy-start(f32[1024]{0:T(1024)} %param.18) | copy-start | bytes 12292
  119.6 108.7 %copy-start.11 = (f32[1024]{0:T(1024)S(1)}, f32[1024]{0:T(1024)}, u32[]{:S(2)}) copy-start(f32[1024]{0:T(1024)} %param.19) | copy-start | bytes 12292
  228.3 4.8 copy-start.3
  231.5 13.8 %copy-start.6 = (bf16[128,1024]{1,0:T(8,128)(2,1)}, bf16[128,1024]{1,0:T(8,128)(2,1)S(1)}, u32[]{:S(2)}) copy-start(bf16[128,1024]{1,0:T(8,128)(2,1)S(1)} %get-tuple-element.49) | copy-start | bytes 786436
  231.5 13.5 %copy-start.10 = (f32[128,2]{0,1:T(2,128)S(1)}, f32[128,2]{0,1:T(2,128)}, u32[]{:S(2)}) copy-start(f32[128,2]{0,1:T(2,128)} %param.14) | copy-start | bytes 3076
  231.5 13.6 %copy-start.12 = (s32[128]{0:T(128)S(1)}, s32[128]{0:T(128)}, u32[]{:S(2)}) copy-start(s32[128]{0:T(128)} %param.15) | copy-start | bytes 1540
  231.5 13.6 %copy-start.5 = (bf16[128,1024]{1,0:T(8,128)(2,1)S(1)}, bf16[128,1024]{1,0:T(8,128)(2,1)}, u32[]{:S(2)}) copy-start(bf16[128,1024]{1,0:T(8,128)(2,1)} %param.12) | copy-start | bytes 786436
  233.1 42.2 %all-to-all-start = ((bf16[128,3,1024]{2,1,0:T(4,128)(2,1)}), bf16[128,3,1024]{2,1,0:T(4,128)(2,1)S(1)}, u32[]{:S(2)}, u32[]{:S(2)}) async-start(bf16[128,3,1024]{2,1,0:T(4,128)(2,1)} %reshape.110), calls=%async_computation | async-start | bytes 2097152 | tf_op jit(solution)/shard_map/all_to_all | solution.py:61
  275.3 37.0 %all-to-all-start.2 = ((bf16[128,3,1024]{2,1,0:T(4,128)(2,1)}), bf16[128,3,1024]{2,1,0:T(4,128)(2,1)}, u32[]{:S(2)}, u32[]{:S(2)}) async-start(bf16[128,3,1024]{2,1,0:T(4,128)(2,1)} %reshape.112), calls=%async_computation.2 | async-start | bytes 2097152 | tf_op jit(solution)/shard_map/all_to_all | solution.py:90
  312.3 5.9 copy-start
  318.3 1.8 copy-start.14
  321.8 35.9 %all-to-all-start.3 = ((bf16[128,3,1024]{2,1,0:T(4,128)(2,1)}), bf16[128,3,1024]{2,1,0:T(4,128)(2,1)S(1)}, u32[]{:S(2)}, u32[]{:S(2)}) async-start(bf16[128,3,1024]{2,1,0:T(4,128)(2,1)} %copy.68), calls=%async_computation.3 | async-start | bytes 2097152 | tf_op jit(solution)/shard_map/all_to_all | solution.py:97
  328.7 46.0 %reduce-scatter.5.cloned.1.call-start = ((), (), s32[]{:S(2)}) async-start(), calls=%async_computation.10 | async-start | bytes 3145728 | tf_op jit(solution)/shard_map/reduce_scatter | solution.py:127
  358.4 3.1 copy-start.4
  365.0 29.0 %reduce-scatter.7.cloned.1.call-start = ((), (), s32[]{:S(2)}) async-start(), calls=%async_computation.11 | async-start | bytes 3145728 | tf_op jit(solution)/shard_map/reduce_scatter | solution.py:130
  365.0 29.1 %copy-start.15 = (bf16[128,3,2048]{2,0,1:T(8,128)(2,1)S(1)}, bf16[128,3,2048]{2,0,1:T(8,128)(2,1)}, u32[]{:S(2)}) copy-start(bf16[128,3,2048]{2,0,1:T(8,128)(2,1)} %copy-done.14) | copy-start | bytes 4718596
  367.1 445.3 %all-reduce.7.cloned.1.call-start = ((), (), s32[]{:S(2)}) async-start(), calls=%async_computation.16 | async-start | bytes 4194304 | tf_op jit(solution)/shard_map/psum | solution.py:140
  394.0 422.9 %reduce-scatter.9.cloned.1.call-start = ((), (), s32[]{:S(2)}) async-start(), calls=%async_computation.12 | async-start | bytes 6291456 | tf_op jit(solution)/shard_map/reduce_scatter | solution.py:103
  398.0 1.9 copy-start.2
  398.0 418.9 %reduce-scatter.11.cloned.1.call-start = ((), (), s32[]{:S(2)}) async-start(), calls=%async_computation.13 | async-start | bytes 6291456 | tf_op jit(solution)/shard_map/reduce_scatter | solution.py:106
  409.7 15.5 %copy-start.13 = (u32[256]{0:T(256)S(1)}, u32[256]{0:T(256)}, u32[]{:S(2)}) copy-start(u32[256]{0:T(256)} %constant.36) | copy-start | bytes 3076
  411.4 48.5 %all-to-all-start.1 = ((bf16[128,3,1024]{2,1,0:T(4,128)(2,1)}), bf16[128,3,1024]{2,1,0:T(4,128)(2,1)S(1)}, u32[]{:S(2)}, u32[]{:S(2)}) async-start(bf16[128,3,1024]{2,1,0:T(4,128)(2,1)} %copy.65), calls=%async_computation.1 | async-start | bytes 2097152 | tf_op jit(solution)/shard_map/all_to_all | solution.py:71
  460.6 351.0 %copy-start.7 = (bf16[128,1024]{1,0:T(8,128)(2,1)S(1)}, bf16[128,1024]{1,0:T(8,128)(2,1)}, u32[]{:S(2)}) copy-start(bf16[128,1024]{1,0:T(8,128)(2,1)} %copy-done.6) | copy-start | bytes 786436
Sparse Core Ops, SparseCore 0:
  11.7 105.3 all-gather.10
  120.8 103.0 all-gather.12
  225.7 18.2 all-gather.6
  245.7 20.2 all-gather.8
  365.1 9.5 reduce-scatter.4
  377.6 16.3 reduce-scatter.6
  399.6 236.3 all-reduce.6
  639.1 14.6 reduce-scatter.8
  657.0 18.7 reduce-scatter.10
where the time goes:
time: 824 us; the launch traced here: 823 us
  waiting for transfers between devices  351 us (43%)
  blocking collectives  348 us (42%)
  starting transfers between devices  41.2 us (5%)
  matrix products  35.6 us (4%)
  local copies, waits for them, and re-layouts  27.4 us (3%)
  between operations  14.9 us (2%)
    psum x1, blocking collectives, body(): summed = lax.psum((halves[0], halves[1], halves[2], halves[3]), 'dp')  345 us
    all_gather x1, waiting for transfers between devices, body(): lax.all_gather(cross_weight, ('dp', 'rep'), axis=0, tiled=True)  106 us
    all_gather x1, waiting for transfers between devices, body(): lax.all_gather(gate_weight, ('dp', 'rep'), axis=0, tiled=True)  104 us
    all_to_all x1, waiting for transfers between devices, body(): lax.all_to_all(expert_result, 'dp', split_axis=0, concat_axis=0, tiled=True)  33.4 us
    all_to_all x1, waiting for transfers between devices, body(): lax.all_to_all(back_rows, 'dp', split_axis=0, concat_axis=0, tiled=True)  28.5 us
    all_to_all x1, waiting for transfers between devices, body(): lax.all_to_all(send_buffer, 'dp', split_axis=0, concat_axis=0, tiled=True)  27.1 us
    all_to_all x1, waiting for transfers between devices, body(): lax.all_to_all(grad_send, 'dp', split_axis=0, concat_axis=0, tiled=True)  22.5 us
    reduce_scatter x1, waiting for transfers between devices, body(): lax.psum_scatter(weight_gate.astype(jnp.bfloat16), 'rep', scatter_dimensi...  19.3 us
  transfers between devices with their start and end apart: 13, of which 8 were waited for; matrix products, arithmetic and copies ran while one was open for 6% of the time, Pallas kernels for 0%

commit v1 on v0

--- a/solution.py
+++ b/solution.py
@@ -40,7 +40,12 @@
     )
     gate_acc = jnp.dot(
         features,
-        lax.all_gather(gate_weight, ("dp", "rep"), axis=0, tiled=True),
+        jnp.concatenate(
+            lax.all_to_all(
+                jnp.stack([gate_weight] * lax.axis_size(("dp", "rep"))), ("dp", "rep"), 0, 0
+            ),
+            axis=0,
+        ),
         preferred_element_type=jnp.float32,
     )
     cross_term = cross_acc + cross_bias

time: 824 us -> 726 us (0.88)
  waiting for transfers between devices: 351 us -> 234 us
  starting transfers between devices: 41.2 us -> 55.7 us
    all_gather x1 -> x0, waiting for transfers between devices: 104 us -> none  [body(): lax.all_gather(gate_weight, ('dp', 'rep'), axis=0, tiled=True)]
    all_to_all x0 -> x1, starting transfers between devices: none -> 14.6 us  [body(): lax.all_to_all(jnp.stack([gate_weight] * lax.axis_size(('dp', 'rep'))), (...]
    all_gather x1, waiting for transfers between devices: 106 us -> 93.3 us  [body(): lax.all_gather(cross_weight, ('dp', 'rep'), axis=0, tiled=True)]
  transfers between devices with their start and end apart: 13 -> 13, of which waited for: 8 -> 7; matrix products, arithmetic and copies ran while one was open for 6% -> 7% of each run, Pallas kernels for 0% -> 0%
where the time goes in v1:
time: 726 us; the launch traced here: 725 us
  blocking collectives  347 us (48%)
  waiting for transfers between devices  234 us (32%)
  starting transfers between devices  55.7 us (8%)
  matrix products  37.2 us (5%)
  local copies, waits for them, and re-layouts  29.4 us (4%)
  between operations  15.2 us (2%)
    psum x1, blocking collectives, body(): summed = lax.psum((halves[0], halves[1], halves[2], halves[3]), 'dp')  345 us
    all_gather x1, waiting for transfers between devices, body(): lax.all_gather(cross_weight, ('dp', 'rep'), axis=0, tiled=True)  93.3 us
    all_to_all x1, waiting for transfers between devices, body(): lax.all_to_all(expert_result, 'dp', split_axis=0, concat_axis=0, tiled=True)  33.7 us
    all_to_all x1, waiting for transfers between devices, body(): lax.all_to_all(back_rows, 'dp', split_axis=0, concat_axis=0, tiled=True)  28.5 us
    all_to_all x1, waiting for transfers between devices, body(): lax.all_to_all(send_buffer, 'dp', split_axis=0, concat_axis=0, tiled=True)  27.1 us
    all_to_all x1, waiting for transfers between devices, body(): lax.all_to_all(grad_send, 'dp', split_axis=0, concat_axis=0, tiled=True)  22.5 us
    reduce_scatter x1, waiting for transfers between devices, body(): lax.psum_scatter(weight_gate.astype(jnp.bfloat16), 'rep', scatter_dimensi...  19.3 us
    all_to_all x1, starting transfers between devices, body(): lax.all_to_all(jnp.stack([gate_weight] * lax.axis_size(('dp', 'rep'))), (...  14.6 us
  transfers between devices with their start and end apart: 13, of which 7 were waited for; matrix products, arithmetic and copies ran while one was open for 7% of the time, Pallas kernels for 0%

profile of v1, /device:TPU:0, one launch (start us, length us, event | category | flops | bytes accessed | tf_op | source)
XLA Modules:
  0.0 724.5 jit_solution(18181867013735243908)
XLA Ops:
  7.2 0.7 all-gather.9.cloned.1.call-update
  7.9 0.7 all-gather.5.cloned.1.call-update
  8.6 2.6 stack.2
  11.2 14.6 %all-to-all-start = ((bf16[256,4,1024]{2,1,0:T(4,128)(2,1)}), bf16[256,4,1024]{2,1,0:T(4,128)(2,1)S(1)}, u32[]{:S(2)}, u32[]{:S(2)}) async-start(bf16[256,4,1024]{2,1,0:T(4,128)(2,1)} %stack.2), calls=%async_computation | async-start | bytes 4194304 | tf_op jit(solution)/shard_map/all_to_all | solution.py:44
  25.9 0.7 all-gather.7.cloned.1.call-update
  26.6 0.1 copy.58
  26.7 0.1 eq.49
  26.8 0.1 eq.45
  27.0 0.1 copy.61
  27.1 0.2 fusion.30
  27.4 0.2 fusion.31
  27.6 0.1 reduce_sum.68
  27.9 93.3 %all-gather.9.cloned.1.call-done = bf16[256,4,1024]{2,1,0:T(4,128)(2,1)} async-done(((bf16[1,4,1024]{2,1,0:T(4,128)(2,1)}), bf16[256,4,1024]{2,1,0:T(4,128)(2,1)}) %all-gather.9.cloned.1.call-update) | async-done | bytes 2097168 | tf_op jit(solution)/shard_map/all_gather | solution.py:38
  121.2 3.9 reshape.139
  125.1 2.0 reshape.114
  127.2 2.0 convolution_add_fusion.1
  129.2 3.1 fusion.25
  132.3 0.4 convolution_convert_fusion.1
  132.7 1.3 reshape.116
  134.0 11.8 %all-to-all-start.1 = ((bf16[128,3,1024]{2,1,0:T(4,128)(2,1)}), bf16[128,3,1024]{2,1,0:T(4,128)(2,1)S(1)}, u32[]{:S(2)}, u32[]{:S(2)}) async-start(bf16[128,3,1024]{2,1,0:T(4,128)(2,1)} %reshape.116), calls=%async_computation.1 | async-start | bytes 2097152 | tf_op jit(solution)/shard_map/all_to_all | solution.py:66
  145.9 0.1 copy.57
  146.1 0.4 mul.120
  146.5 0.7 mul.121
  147.2 0.1 mul.118
  147.3 0.5 convolution_convert_fusion
  147.8 1.3 reshape.118
  149.1 27.1 %all-to-all-done.1 = bf16[128,3,1024]{2,1,0:T(4,128)(2,1)S(1)} async-done(((bf16[128,3,1024]{2,1,0:T(4,128)(2,1)}), bf16[128,3,1024]{2,1,0:T(4,128)(2,1)S(1)}, u32[]{:S(2)}, u32[]{:S(2)}) %all-to-all-start.1) | async-done | bytes 786464 | tf_op jit(solution)/shard_map/all_to_all | solution.py:66
  176.2 7.9 %all-to-all-start.3 = ((bf16[128,3,1024]{2,1,0:T(4,128)(2,1)}), bf16[128,3,1024]{2,1,0:T(4,128)(2,1)}, u32[]{:S(2)}, u32[]{:S(2)}) async-start(bf16[128,3,1024]{2,1,0:T(4,128)(2,1)} %reshape.118), calls=%async_computation.3 | async-start | bytes 2097152 | tf_op jit(solution)/shard_map/all_to_all | solution.py:95
  184.1 0.8 copy.69
  185.0 5.7 fusion.6
  190.7 22.5 %all-to-all-done.3 = bf16[128,3,1024]{2,1,0:T(4,128)(2,1)} async-done(((bf16[128,3,1024]{2,1,0:T(4,128)(2,1)}), bf16[128,3,1024]{2,1,0:T(4,128)(2,1)}, u32[]{:S(2)}, u32[]{:S(2)}) %all-to-all-start.3) | async-done | bytes 786464 | tf_op jit(solution)/shard_map/all_to_all | solution.py:95
  213.2 5.9 multiply_convert_fusion
  219.1 1.8 fusion.12
  221.0 1.6 copy.68
  222.6 7.0 all-to-all-start.4
  229.6 0.3 reduce-scatter.5.cloned.1.call-start
  229.9 0.1 mul.110
  230.0 28.5 %all-to-all-done.4 = bf16[128,3,1024]{2,1,0:T(4,128)(2,1)S(1)} async-done(((bf16[128,3,1024]{2,1,0:T(4,128)(2,1)}), bf16[128,3,1024]{2,1,0:T(4,128)(2,1)S(1)}, u32[]{:S(2)}, u32[]{:S(2)}) %all-to-all-start.4) | async-done | bytes 786464 | tf_op jit(solution)/shard_map/all_to_all | solution.py:102
  258.5 0.7 reshape.119
  259.2 1.2 gather_fusion.1
  260.4 0.7 reshape.121
  261.1 1.2 reduce_sum.72
  262.3 1.4 fusion.35
  263.8 2.1 convert_bitcast_fusion.1
  265.9 2.1 convert_bitcast_fusion
  268.0 7.6 %reduce-scatter.5.cloned.1.call-done = bf16[512,1024]{0,1:T(8,128)(2,1)} async-done(((bf16[1024,1024]{0,1:T(8,128)(2,1)}), bf16[512,1024]{0,1:T(8,128)(2,1)}) %reduce-scatter.5.cloned.1.call-update) | async-done | bytes 1048592 | tf_op jit(solution)/shard_map/reduce_scatter | solution.py:132
  275.6 19.3 %reduce-scatter.7.cloned.1.call-done = bf16[512,1024]{0,1:T(8,128)(2,1)} async-done(((bf16[1024,1024]{0,1:T(8,128)(2,1)}), bf16[512,1024]{0,1:T(8,128)(2,1)}) %reduce-scatter.7.cloned.1.call-update) | async-done | bytes 1048592 | tf_op jit(solution)/shard_map/reduce_scatter | solution.py:135
  295.0 3.9 fusion.8
  298.9 1.8 copy-done.2
  300.8 5.8 fusion.9
  306.6 4.0 fusion.15
  310.6 1.6 copy.65
  312.3 13.8 %all-to-all-start.2 = ((bf16[128,3,1024]{2,1,0:T(4,128)(2,1)}), bf16[128,3,1024]{2,1,0:T(4,128)(2,1)S(1)}, u32[]{:S(2)}, u32[]{:S(2)}) async-start(bf16[128,3,1024]{2,1,0:T(4,128)(2,1)} %copy.65), calls=%async_computation.2 | async-start | bytes 2097152 | tf_op jit(solution)/shard_map/all_to_all | solution.py:76
  326.1 0.6 dynamic-slice
  327.4 33.7 %all-to-all-done.2 = bf16[128,3,1024]{2,1,0:T(4,128)(2,1)S(1)} async-done(((bf16[128,3,1024]{2,1,0:T(4,128)(2,1)}), bf16[128,3,1024]{2,1,0:T(4,128)(2,1)S(1)}, u32[]{:S(2)}, u32[]{:S(2)}) %all-to-all-start.2) | async-done | bytes 786464 | tf_op jit(solution)/shard_map/all_to_all | solution.py:76
  361.0 0.7 reshape.117
  361.7 1.2 gather_fusion
  362.9 0.7 reshape.120
  363.5 2.5 all-reduce.4
  366.1 344.9 %all-reduce.2 = (f32[512]{0:T(512)}, f32[512]{0:T(512)}) all-reduce(f32[512]{0:T(512)S(1)} %get-tuple-element.52, f32[512]{0:T(512)S(1)} %get-tuple-element.51), channel_id=1, replica_groups=mesh['dp'=128,'rep'=2] {'dp'}, use_global_device_ids=true, to_apply=%region_12.13 | all-reduce | flops 1024 | bytes 8192 | tf_op jit(solution)/shard_map/psum | solution.py:145
  711.0 1.3 multiply_reduce_fusion
  712.4 0.8 add_convert_fusion
  713.2 2.3 copy.72
  715.4 2.3 copy.73
  (63 shorter events, 0.9 us)
Async XLA Ops:
  7.2 114.0 %all-gather.9.cloned.1.call-start = ((), (), s32[]{:S(2)}) async-start(), calls=%async_computation.15 | async-start | bytes 2105344 | tf_op jit(solution)/shard_map/all_gather | solution.py:38
  7.9 177.1 %all-gather.5.cloned.1.call-start = ((), (), s32[]{:S(2)}) async-start(), calls=%async_computation.9 | async-start | bytes 6291456 | tf_op jit(solution)/shard_map/all_gather | solution.py:61
  11.2 15.3 %copy-start.9 = (s32[128,2]{0,1:T(2,128)S(1)}, s32[128,2]{0,1:T(2,128)}, u32[]{:S(2)}) copy-start(s32[128,2]{0,1:T(2,128)} %param.13) | copy-start | bytes 3076
  11.2 113.9 %all-to-all-start = ((bf16[256,4,1024]{2,1,0:T(4,128)(2,1)}), bf16[256,4,1024]{2,1,0:T(4,128)(2,1)S(1)}, u32[]{:S(2)}, u32[]{:S(2)}) async-start(bf16[256,4,1024]{2,1,0:T(4,128)(2,1)} %stack.2), calls=%async_computation | async-start | bytes 4194304 | tf_op jit(solution)/shard_map/all_to_all | solution.py:44
  25.8 187.4 %all-gather.7.cloned.1.call-start = ((), (), s32[]{:S(2)}) async-start(), calls=%async_computation.10 | async-start | bytes 6291456 | tf_op jit(solution)/shard_map/all_gather | solution.py:62
  27.9 99.2 %copy-start.1 = (bf16[128,1024]{1,0:T(8,128)(2,1)S(1)}, bf16[128,1024]{1,0:T(8,128)(2,1)}, u32[]{:S(2)}) copy-start(bf16[128,1024]{1,0:T(8,128)(2,1)} %param.11) | copy-start | bytes 786436
  27.9 99.2 %copy-start.8 = (f32[1024]{0:T(1024)S(1)}, f32[1024]{0:T(1024)}, u32[]{:S(2)}) copy-start(f32[1024]{0:T(1024)} %param.18) | copy-start | bytes 12292
  125.1 4.1 copy-start.11
  129.2 3.1 copy-start.3
  132.3 1.7 copy-start.6
  132.3 13.5 %copy-start.10 = (f32[128,2]{0,1:T(2,128)S(1)}, f32[128,2]{0,1:T(2,128)}, u32[]{:S(2)}) copy-start(f32[128,2]{0,1:T(2,128)} %param.14) | copy-start | bytes 3076
  132.3 13.6 %copy-start.12 = (s32[128]{0:T(128)S(1)}, s32[128]{0:T(128)}, u32[]{:S(2)}) copy-start(s32[128]{0:T(128)} %param.15) | copy-start | bytes 1540
  132.3 13.6 %copy-start.5 = (bf16[128,1024]{1,0:T(8,128)(2,1)S(1)}, bf16[128,1024]{1,0:T(8,128)(2,1)}, u32[]{:S(2)}) copy-start(bf16[128,1024]{1,0:T(8,128)(2,1)} %param.12) | copy-start | bytes 786436
  134.0 42.2 %all-to-all-start.1 = ((bf16[128,3,1024]{2,1,0:T(4,128)(2,1)}), bf16[128,3,1024]{2,1,0:T(4,128)(2,1)S(1)}, u32[]{:S(2)}, u32[]{:S(2)}) async-start(bf16[128,3,1024]{2,1,0:T(4,128)(2,1)} %reshape.116), calls=%async_computation.1 | async-start | bytes 2097152 | tf_op jit(solution)/shard_map/all_to_all | solution.py:66
  176.2 37.0 %all-to-all-start.3 = ((bf16[128,3,1024]{2,1,0:T(4,128)(2,1)}), bf16[128,3,1024]{2,1,0:T(4,128)(2,1)}, u32[]{:S(2)}, u32[]{:S(2)}) async-start(bf16[128,3,1024]{2,1,0:T(4,128)(2,1)} %reshape.118), calls=%async_computation.3 | async-start | bytes 2097152 | tf_op jit(solution)/shard_map/all_to_all | solution.py:95
  213.2 5.9 copy-start
  219.1 1.8 copy-start.14
  222.6 35.9 %all-to-all-start.4 = ((bf16[128,3,1024]{2,1,0:T(4,128)(2,1)}), bf16[128,3,1024]{2,1,0:T(4,128)(2,1)S(1)}, u32[]{:S(2)}, u32[]{:S(2)}) async-start(bf16[128,3,1024]{2,1,0:T(4,128)(2,1)} %copy.68), calls=%async_computation.4 | async-start | bytes 2097152 | tf_op jit(solution)/shard_map/all_to_all | solution.py:102
  229.6 46.0 %reduce-scatter.5.cloned.1.call-start = ((), (), s32[]{:S(2)}) async-start(), calls=%async_computation.11 | async-start | bytes 3145728 | tf_op jit(solution)/shard_map/reduce_scatter | solution.py:132
  259.2 3.1 copy-start.4
  265.8 29.0 %reduce-scatter.7.cloned.1.call-start = ((), (), s32[]{:S(2)}) async-start(), calls=%async_computation.12 | async-start | bytes 3145728 | tf_op jit(solution)/shard_map/reduce_scatter | solution.py:135
  265.9 29.1 %copy-start.15 = (bf16[128,3,2048]{2,0,1:T(8,128)(2,1)S(1)}, bf16[128,3,2048]{2,0,1:T(8,128)(2,1)}, u32[]{:S(2)}) copy-start(bf16[128,3,2048]{2,0,1:T(8,128)(2,1)} %copy-done.14) | copy-start | bytes 4718596
  268.0 445.2 %all-reduce.7.cloned.1.call-start = ((), (), s32[]{:S(2)}) async-start(), calls=%async_computation.16 | async-start | bytes 4194304 | tf_op jit(solution)/shard_map/psum | solution.py:145
  294.9 422.8 %reduce-scatter.9.cloned.1.call-start = ((), (), s32[]{:S(2)}) async-start(), calls=%async_computation.13 | async-start | bytes 6291456 | tf_op jit(solution)/shard_map/reduce_scatter | solution.py:108
  298.9 1.9 copy-start.2
  298.9 418.8 %reduce-scatter.11.cloned.1.call-start = ((), (), s32[]{:S(2)}) async-start(), calls=%async_computation.14 | async-start | bytes 6291456 | tf_op jit(solution)/shard_map/reduce_scatter | solution.py:111
  310.6 15.5 %copy-start.13 = (u32[256]{0:T(256)S(1)}, u32[256]{0:T(256)}, u32[]{:S(2)}) copy-start(u32[256]{0:T(256)} %constant.36) | copy-start | bytes 3076
  312.3 48.8 %all-to-all-start.2 = ((bf16[128,3,1024]{2,1,0:T(4,128)(2,1)}), bf16[128,3,1024]{2,1,0:T(4,128)(2,1)S(1)}, u32[]{:S(2)}, u32[]{:S(2)}) async-start(bf16[128,3,1024]{2,1,0:T(4,128)(2,1)} %copy.65), calls=%async_computation.2 | async-start | bytes 2097152 | tf_op jit(solution)/shard_map/all_to_all | solution.py:76
  361.7 350.7 %copy-start.7 = (bf16[128,1024]{1,0:T(8,128)(2,1)S(1)}, bf16[128,1024]{1,0:T(8,128)(2,1)}, u32[]{:S(2)}) copy-start(bf16[128,1024]{1,0:T(8,128)(2,1)} %copy-done.6) | copy-start | bytes 786436
Sparse Core Ops, SparseCore 0:
  11.7 109.4 all-gather.8
  123.0 18.2 all-gather.4
  143.1 20.2 all-gather.6
  266.0 9.5 reduce-scatter.4
  278.5 16.3 reduce-scatter.6
  300.3 235.9 all-reduce.6
  539.5 14.7 reduce-scatter.8
  557.4 18.7 reduce-scatter.10
